TPU v7x, 128 devices: a whole 4x4x4 slice. The times are simulated.
128 devices in a mesh: grp: 4 (over x_lo, core), mz: 32 (over y, x_hi, z).
Axes of the slice: x: 4 (x_hi: 2, x_lo: 2; x = x_hi * 2 + x_lo), y: 4, z: 4, core: 2. Of those that a mesh axis runs over, the one named last changes fastest.
Arguments:
- intensities: float32 [512, 8, 131072], P('grp', None, 'mz'), as said below
- sample_start: float32 [512, 256], P('grp'), as said below
- scan_start: float32 [8, 256], replicated, as said below
- mass_start: float32 [131072, 256], P('mz'), as said below
Outputs:
- sample_factor: float32 [512, 256], P('grp')
- scan_factor: float32 [8, 256], replicated
- mass_factor: float32 [131072, 256], P('mz')
Inputs may be any that keep to these rules, and one draw needn't show every extreme that they name: Measured intensities of the cohort. `sample_start`: a starting estimate of the sample factor. `scan_start`: a starting estimate of the scan factor. `mass_start`: a starting estimate of the m/z factor.
All inputs are finite; a program needn't handle non-finite values.
Results may differ from a plain program's by a relative error of at most 0.0001.
Values sent between devices are 32-bit elements; how exact they have to be, the bound alone decides.
A program may use at most 128 MiB of HBM per device.

v0:
```python
import jax
import jax.numpy as jnp
from jax import lax
from jax.sharding import PartitionSpec as P

STEPS = 2


precise = lax.Precision.HIGHEST


def frobenius(gram):
    return jnp.sqrt(jnp.sum(gram * gram) + 1e-12)


def gram_of(factor):
    return jnp.dot(factor.T, factor, precision=precise, preferred_element_type=jnp.float32)


def descend(factor, hessian, drive):
    product = jnp.dot(factor, hessian, precision=precise, preferred_element_type=jnp.float32)
    return factor - (product - drive) / frobenius(hessian)


def local(intensities, sample_start, scan_start, mass_start):
    factor_a = sample_start
    factor_b = scan_start
    factor_c = mass_start
    samples_here = intensities.shape[0]
    scans_here = intensities.shape[1]
    bins_here = intensities.shape[2]
    rank_width = factor_a.shape[1]
    unfolded = intensities.reshape(samples_here * scans_here, bins_here)
    for iteration in range(STEPS):
        gram_a = lax.psum(gram_of(factor_a), "grp")
        gram_b = gram_of(factor_b)
        gram_c = lax.psum(gram_of(factor_c), "mz")
        contracted = jnp.einsum("ijk,kr->ijr", intensities, factor_c, precision=precise)
        drive_a = lax.psum(jnp.einsum("ijr,jr->ir", contracted, factor_b, precision=precise), "mz")
        drive_b = lax.psum(
            jnp.einsum("ijr,ir->jr", contracted, factor_a, precision=precise), ("grp", "mz")
        )
        khatri_rao = (factor_a[:, None, :] * factor_b[None, :, :]).reshape(
            samples_here * scans_here, rank_width
        )
        hessian_a = gram_b * gram_c
        hessian_b = gram_a * gram_c
        hessian_c = gram_a * gram_b
        partial_c = lax.dot_general(
            unfolded,
            khatri_rao,
            (((0,), (0,)), ((), ())),
            precision=precise,
            preferred_element_type=jnp.float32,
        )
        drive_c = lax.psum(partial_c, "grp")
        new_c = descend(factor_c, hessian_c, drive_c)
        new_a = descend(factor_a, hessian_a, drive_a)
        new_b = descend(factor_b, hessian_b, drive_b)
        factor_a, factor_b, factor_c = (new_a, new_b, new_c)
    return (factor_a, factor_b, factor_c)


def solution(mesh):
    placed = (P("grp", None, "mz"), P("grp", None), P(), P("mz", None))
    return jax.shard_map(
        local,
        mesh=mesh,
        in_specs=placed,
        out_specs=(P("grp", None), P(), P("mz", None)),
        check_vma=False,
    )
```

profile of v0, /device:TPU:1, one launch (start us, length us, event | category | flops | bytes accessed | tf_op | source)
XLA Modules:
  0.0 1056.7 jit_solution(8836801280862759096)
XLA Ops:
  7.2 11.1 %fusion.53 = f32[256,256]{1,0:T(8,128)} fusion(f32[4096,256]{1,0:T(8,128)} %param.7), kind=kOutput, calls=%fused_computation.59 | convolution fusion | flops 3221225472 | bytes 4456448 | tf_op jit(solution)/shard_map/dot_general | solution.py:17
  18.3 16.7 %fusion.18 = f32[128,8,256]{2,1,0:T(8,128)S(1)} fusion(f32[128,8,4096]{2,1,0:T(8,128)} %param.4, f32[4096,256]{1,0:T(8,128)S(1)} %copy-done), kind=kOutput, calls=%fused_computation.16 | convolution fusion | flops 12884901888 | bytes 22020096 | tf_op jit(solution)/shard_map/ijk,kr->ijr/dot_general | solution.py:38
  35.0 0.3 fusion.36
  35.3 0.8 copy.26
  36.1 0.3 all-reduce.16.cloned.1.call-start
  36.5 28.8 %fusion.7 = f32[4096,256]{0,1:T(8,128)} fusion(f32[128,8,4096]{2,1,0:T(8,128)} %param.4, f32[8,256]{1,0:T(8,128)S(1)} %copy-done.6, f32[128,256]{0,1:T(8,128)S(1)} %copy.8), kind=kOutput, calls=%fused_computation.9 | convolution fusion | flops 12885164032 | bytes 21110784 | tf_op jit(solution)/shard_map/dot_general | solution.py:49
  65.3 1.1 fusion.54
  66.4 0.4 all-reduce.10.cloned.1.call-start
  66.9 5.7 copy.11
  72.6 0.3 fusion.35
  72.9 286.1 %all-reduce.12.cloned.1.call-done = (f32[128,256]{0,1:T(8,128)}, f32[256,256]{1,0:T(8,128)}) async-done(((f32[128,256]{0,1:T(8,128)}, f32[256,256]{1,0:T(8,128)}), (f32[128,256]{0,1:T(8,128)}, f32[256,256]{1,0:T(8,128)})) %all-reduce.12.cloned.1.call-update) | async-done | bytes 393232 | tf_op jit(solution)/shard_map/psum | solution.py:39
  359.0 115.0 %all-reduce.16.cloned.1.call-done = (f32[256,256]{1,0:T(8,128)}, f32[4096,256]{0,1:T(8,128)}) async-done(((f32[256,256]{1,0:T(8,128)}, f32[4096,256]{0,1:T(8,128)}), (f32[256,256]{1,0:T(8,128)}, f32[4096,256]{0,1:T(8,128)})) %all-reduce.16.cloned.1.call-update) | async-done | bytes 4456464 | tf_op jit(solution)/shard_map/psum | solution.py:35
  474.0 2.1 multiply_reduce_fusion.3
  476.8 11.9 %fusion.14 = f32[4096,256]{0,1:T(8,128)S(1)} fusion(f32[4096,256]{0,1:T(8,128)} %copy.11, f32[4096,256]{0,1:T(8,128)} %get-tuple-element.21, f32[4096,256]{1,0:T(8,128)} %param.7, f32[]{:T(128)S(6)} %sqrt.20, f32[256,256]{1,0:T(8,128)} %get-tuple-element.20, f32[256,256]{1,0:T(8,128)S(1)} %get-tuple-element.22), kind=kOutput, calls=%fused_computation.12 | convolution fusion | flops 3224436736 | bytes 17301508 | tf_op jit(solution)/shard_map/dot_general | solution.py:21
  488.8 4.3 fusion.55
  493.0 28.1 %fusion.20 = f32[128,8,256]{0,2,1:T(8,128)S(1)} fusion(f32[128,8,4096]{2,1,0:T(8,128)} %param.4, f32[4096,256]{0,1:T(8,128)S(1)} %fusion.14), kind=kOutput, calls=%fused_computation.18 | convolution fusion | flops 12884901888 | bytes 22020096 | tf_op jit(solution)/shard_map/ijk,kr->ijr/dot_general | solution.py:38
  522.5 0.6 fusion.29
  523.1 2.3 fusion.39
  525.5 66.3 %all-reduce = (f32[8,256]{1,0:T(8,128)S(1)}, f32[8,256]{1,0:T(8,128)S(1)}) all-reduce(f32[8,256]{1,0:T(8,128)S(1)} %bitcast.90, f32[8,256]{1,0:T(8,128)S(1)} %bitcast.91), channel_id=1, replica_groups=mesh['grp'=4,'mz'=32] {'grp','mz'}, use_global_device_ids=true, to_apply=%region_4.0 | all-reduce | flops 4096 | bytes 32768 | tf_op jit(solution)/shard_map/psum | solution.py:40
  591.7 0.2 fusion.34
  592.0 0.1 copy.34
  592.1 3.0 fusion.41
  595.2 29.0 %fusion.10 = f32[4096,256]{0,1:T(8,128)} fusion(f32[128,8,4096]{2,1,0:T(8,128)} %param.4, f32[8,256]{1,0:T(8,128)S(1)} %fusion.34, f32[128,256]{0,1:T(8,128)S(1)} %fusion.29), kind=kOutput, calls=%fused_computation.10 | convolution fusion | flops 12885164032 | bytes 21110784 | tf_op jit(solution)/shard_map/dot_general | solution.py:49
  624.2 1.1 fusion.56
  625.3 285.8 %all-reduce.10.cloned.1.call-done = (f32[128,256]{0,1:T(8,128)}, f32[256,256]{1,0:T(8,128)}) async-done(((f32[128,256]{0,1:T(8,128)}, f32[256,256]{1,0:T(8,128)}), (f32[128,256]{0,1:T(8,128)}, f32[256,256]{1,0:T(8,128)})) %all-reduce.10.cloned.1.call-update) | async-done | bytes 393232 | tf_op jit(solution)/shard_map/psum | solution.py:39
  911.1 114.7 %all-reduce.14.cloned.1.call-done = (f32[256,256]{1,0:T(8,128)}, f32[4096,256]{0,1:T(8,128)}) async-done(((f32[256,256]{1,0:T(8,128)}, f32[4096,256]{0,1:T(8,128)}), (f32[256,256]{1,0:T(8,128)}, f32[4096,256]{0,1:T(8,128)})) %all-reduce.14.cloned.1.call-update) | async-done | bytes 4456464 | tf_op jit(solution)/shard_map/psum | solution.py:35
  1025.8 2.1 multiply_reduce_fusion
  1029.9 1.6 fusion.26
  1031.5 0.8 copy.16
  1032.3 11.0 %fusion.16 = f32[4096,256]{0,1:T(8,128)} fusion(f32[4096,256]{0,1:T(8,128)} %copy-done.1, f32[4096,256]{0,1:T(8,128)} %get-tuple-element.19, f32[]{:T(128)S(6)} %sqrt.23, f32[256,256]{1,0:T(8,128)} %get-tuple-element.18, f32[256,256]{1,0:T(8,128)S(1)} %get-tuple-element.23), kind=kOutput, calls=%fused_computation.14 | convolution fusion | flops 3224436736 | bytes 13107204 | tf_op jit(solution)/shard_map/dot_general | solution.py:21
  1043.3 5.7 copy.17
  1048.9 0.8 fusion.31
  (26 shorter events, 0.3 us)
Async XLA Ops:
  7.2 351.9 %all-reduce.12.cloned.1.call-start = ((), (), s32[]{:S(2)}) async-start(), calls=%async_computation.1 | async-start | bytes 786432 | tf_op jit(solution)/shard_map/psum | solution.py:39
  7.2 11.1 %copy-start = (f32[4096,256]{1,0:T(8,128)S(1)}, f32[4096,256]{1,0:T(8,128)}, u32[]{:S(2)}) copy-start(f32[4096,256]{1,0:T(8,128)} %param.7) | copy-start | bytes 12582916
  18.3 16.7 %copy-start.6 = (f32[8,256]{1,0:T(8,128)S(1)}, f32[8,256]{1,0:T(8,128)}, u32[]{:S(2)}) copy-start(f32[8,256]{1,0:T(8,128)} %param.6) | copy-start | bytes 24580
  18.3 18.1 %copy-start.2 = (f32[128,256]{1,0:T(8,128)S(1)}, f32[128,256]{1,0:T(8,128)}, u32[]{:S(2)}) copy-start(f32[128,256]{1,0:T(8,128)} %param.5) | copy-start | bytes 393220
  36.1 437.9 %all-reduce.16.cloned.1.call-start = ((), (), s32[]{:S(2)}) async-start(), calls=%async_computation.3 | async-start | bytes 8912896 | tf_op jit(solution)/shard_map/psum | solution.py:35
  66.4 844.6 %all-reduce.10.cloned.1.call-start = ((), (), s32[]{:S(2)}) async-start(), calls=%async_computation | async-start | bytes 786432 | tf_op jit(solution)/shard_map/psum | solution.py:39
  488.7 4.3 copy-start.1
  493.0 29.5 %copy-start.5 = (f32[256,256]{1,0:T(8,128)S(1)}, f32[256,256]{1,0:T(8,128)}, u32[]{:S(2)}) copy-start(f32[256,256]{1,0:T(8,128)} %get-tuple-element.17) | copy-start | bytes 786436
  493.0 29.5 %copy-start.8 = (f32[128,256]{0,1:T(8,128)S(1)}, f32[128,256]{0,1:T(8,128)}, u32[]{:S(2)}) copy-start(f32[128,256]{0,1:T(8,128)} %get-tuple-element.16) | copy-start | bytes 393220
  493.0 98.7 %copy-start.3 = (f32[256,256]{1,0:T(8,128)S(1)}, f32[256,256]{1,0:T(8,128)}, u32[]{:S(2)}) copy-start(f32[256,256]{1,0:T(8,128)} %get-tuple-element.20) | copy-start | bytes 786436
  595.1 430.6 %all-reduce.14.cloned.1.call-start = ((), (), s32[]{:S(2)}) async-start(), calls=%async_computation.2 | async-start | bytes 8912896 | tf_op jit(solution)/shard_map/psum | solution.py:35
  1043.3 5.7 copy-start.4
  1043.3 5.7 copy-start.7
Sparse Core Ops, SparseCore 0:
  36.2 322.7 all-reduce.11
  362.4 111.6 all-reduce.15
  595.3 315.7 all-reduce.9
  914.1 111.6 all-reduce.13
where the time goes:
time: 1060 us
  waiting for transfers between devices  802 us (76%)
  matrix products  156 us (15%)
  blocking collectives  66.3 us (6%)
  between operations  18.5 us (2%)
  local copies, waits for them, and re-layouts  13.2 us (1%)
    psum x2, waiting for transfers between devices, local(): lax.psum(jnp.einsum('ijr,jr->ir', contracted, factor_b, precision=precise...  572 us
    psum x2, waiting for transfers between devices, local(): gram_a = lax.psum(gram_of(factor_a), 'grp')  230 us
    psum x1, blocking collectives, local(): lax.psum(jnp.einsum('ijr,ir->jr', contracted, factor_a, precision=precise...  66.3 us
    dot_general x2, matrix products, local(): lax.dot_general(unfolded, khatri_rao, (((0,), (0,)), ((), ())), precision...  57.8 us
    dot_general x2, matrix products, local(): jnp.einsum('ijk,kr->ijr', intensities, factor_c, precision=precise)  44.8 us
    dot_general x6, matrix products, descend(): jnp.dot(factor, hessian, precision=precise, preferred_element_type=jnp.fl...  26.2 us
    dot_general x6, matrix products, gram_of(): jnp.dot(factor.T, factor, precision=precise, preferred_element_type=jnp.f...  21.7 us
  transfers between devices with their start and end apart: 4, of which 4 were waited for; matrix products, arithmetic and copies ran while one was open for 6% of the time, Pallas kernels for 0%

commit v1 on v0

v1 whole, which is shorter than its diff:
```python
import functools

import jax
import jax.numpy as jnp
from jax import lax
from jax.experimental import pallas as pl
from jax.experimental.pallas import tpu as pltpu
from jax.sharding import PartitionSpec as P

MESH = pl.DeviceIdType.MESH
F32 = jnp.float32
BF16 = jnp.bfloat16
STEPS = 2
RANK = 256
SCANS = 8
ROWS = 128
BINS = 4096
CHUNKS = 16
WIDE = BINS // CHUNKS
HALF = WIDE // 2
FIRST = 8
SECOND = 10
THIRD = 10
PIECE = 72


def split(x):
    high = x.astype(BF16)
    return high, (x - high.astype(F32)).astype(BF16)


def contract(a, b, i, j, precision=None):
    return lax.dot_general(
        a, b, (((i,), (j,)), ((), ())), precision=precision, preferred_element_type=F32
    )


def contract3(a, b, i, j):
    return contract(a[0], b[0], i, j) + (contract(a[0], b[1], i, j) + contract(a[1], b[0], i, j))


def exact(a, b, i, j):
    return contract(a, b, i, j, lax.Precision.HIGHEST)


def inverse_norm(gram):
    return 1.0 / jnp.sqrt(jnp.sum(gram * gram) + 1e-12)


def kernel(
    t_hbm, a0, b0, c_hbm, out_a, out_b, out_c,
    t, c0, c1, c2, part, from_sib, from_cp, y, krh, krl, gram, a1, b1,
    pc, pa, ma, grama, pa_in, pa_sum, pa_cp, mb_out, mb_in,
    pieces, z_in, y_in, x_out, x_in, mbx_in, ag_in, half_out, half_in,
    t_sem, c_sem, o_sem, sib_s, sib_r, cp_s, cp_r, c1_s, c1_r, c2_s, c2_r, few_s, few_r,
):
    g = lax.axis_index("grp")
    m = lax.axis_index("mz")
    core = lax.rem(g, 2)
    z = lax.rem(m, 4)
    hi = lax.rem(m // 4, 2)
    yy = m // 8
    g_sib = g + 1 - 2 * core
    g_cp = lax.rem(g + 2, 4)
    m_x = m + 4 - 8 * hi
    sib, cp, xp, dg = (g_sib, m), (g_cp, m), (g, m_x), (g_cp, m_x)
    z_to = [(g, m - z + lax.rem(z + k, 4)) for k in (1, 2, 3)]
    y_to = [(g, m + 8 * (lax.rem(yy + k, 4) - yy)) for k in (1, 2, 3)]

    def load_t(i):
        cols = pl.ds(pl.multiple_of(i * WIDE, WIDE), WIDE)
        return pltpu.make_async_copy(t_hbm.at[:, cols], t.at[:, cols], t_sem.at[i])

    load_c = pltpu.make_async_copy(c_hbm, c0, c_sem)
    for i in range(CHUNKS):
        load_t(i).start()
    load_c.start()

    partners = [sib, cp, xp, dg, *z_to, *y_to]
    barrier = pltpu.get_barrier_semaphore()
    for partner in partners:
        pl.semaphore_signal(barrier, inc=1, device_id=partner, device_id_type=MESH)

    def khatri_rao(a, b):
        product = (a[:, None, :] * b[None, :, :]).reshape(ROWS * SCANS, RANK)
        krh[...], krl[...] = split(product)

    def remote(src, dst, send, recv, to):
        return pltpu.make_async_remote_copy(
            src_ref=src, dst_ref=dst, send_sem=send, recv_sem=recv, device_id=to, device_id_type=MESH
        )

    own = pl.ds(pl.multiple_of(core * HALF, HALF), HALF)
    other = pl.ds(pl.multiple_of((1 - core) * HALF, HALF), HALF)

    def to_sib(s, i):
        return remote(part.at[s, i, other], from_sib.at[s, i], sib_s.at[s, i], sib_r.at[s, i], sib)

    def to_cp(s, i):
        return remote(part.at[s, i, own], from_cp.at[s, i], cp_s.at[s, i], cp_r.at[s, i], cp)

    def chunk(i):
        return pl.ds(pl.multiple_of(i * WIDE, WIDE), WIDE)

    def own_rows(i):
        return pl.ds(pl.multiple_of(i * WIDE + core * HALF, HALF), HALF)

    def c1_to_sib(i):
        return remote(c1.at[own_rows(i)], c1.at[own_rows(i)], c1_s.at[i], c1_r.at[i], sib)

    def c2_to_sib(i):
        return remote(c2.at[i], out_c.at[own_rows(i)], c2_s.at[i], c2_r.at[i], sib)

    def c2_out(i):
        return pltpu.make_async_copy(c2.at[i], out_c.at[own_rows(i)], o_sem.at[i])

    def produce(s, i):
        part[s, i] = contract3(split(t[:, chunk(i)]), (krh[...], krl[...]), 0, 0)
        to_sib(s, i).start()

    def forward(s, i):
        to_sib(s, i).wait()
        part[s, i, own] += from_sib[s, i]
        to_cp(s, i).start()

    def run(s, first, last, wait_t=False):
        def body(i, carry):
            if wait_t:
                load_t(i).wait()
            produce(s, i)

            @pl.when(i > first)
            def _():
                forward(s, i - 1)

            return carry

        lax.fori_loop(first, last, body, 0)
        forward(s, last - 1)

    def accumulate(factor, i):
        rows = chunk(i)
        block = split(factor[rows, :])
        y[...] += contract3(split(t[:, rows]), block, 1, 0)
        mine = split(factor[rows, pl.ds(pl.multiple_of(core * 128, 128), 128)])
        gram[...] += contract3(mine, block, 0, 0)

    def update_c(s, i, source, hessian, scale):
        to_cp(s, i).wait()
        drive = part[s, i, own] + from_cp[s, i]
        old = source[own_rows(i), :]
        return old - (exact(old, hessian[...], 1, 0) - drive) * scale

    def small_pa(s, a):
        grama[...] = exact(a, a, 0, 0)
        theirs = pl.ds(pl.multiple_of((1 - core) * 128 + z * 32, 32), 32)
        return remote(grama.at[theirs], pa_in.at[s], few_s.at[s, 0], few_r.at[s, 0], sib)

    def small_pa_sum(s):
        mine = pl.ds(pl.multiple_of(core * 128 + z * 32, 32), 32)
        pa_sum[s] = grama[mine, :] + pa_in[s]
        return remote(pa_sum.at[s], pa_cp.at[s], few_s.at[s, 1], few_r.at[s, 1], cp)

    def small_mb(s, a):
        y3 = y[...].reshape(ROWS, SCANS, RANK)
        mb_out[s] = jnp.sum(y3 * a[:, None, :], axis=0)
        return remote(mb_out.at[s], mb_in.at[s], few_s.at[s, 2], few_r.at[s, 2], sib)

    def small_pieces(s, b, mb_copy):
        y3 = y[...].reshape(ROWS, SCANS, RANK)
        drive = jnp.sum(y3 * b[None, :, :], axis=1)
        mb_copy.wait()
        mb = mb_out[s] + mb_in[s]
        for p in range(4):
            pieces[s, p, 0:32, :] = drive[32 * p : 32 * p + 32]
            pieces[s, p, 32:64, :] = gram[32 * p : 32 * p + 32, :]
            pieces[s, p, 64:72, :] = mb
        copies = [
            remote(pieces.at[s, lax.rem(z + k, 4)], z_in.at[s, k], few_s.at[s, 2 + k], few_r.at[s, 2 + k], z_to[k - 1])
            for k in (1, 2, 3)
        ]
        for copy in copies:
            copy.start()
        z_in[s, 0] = pieces[s, z]
        return copies

    def ordered_sum(slots, s, me):
        total = slots[s, me]
        for other_one in (1, 2, 3):
            total = total + slots[s, lax.rem(me + 4 - other_one, 4)]
        return total

    def small_y(s):
        y_in[s, 0] = ordered_sum(z_in, s, z)
        copies = [
            remote(y_in.at[s, 0], y_in.at[s, k], few_s.at[s, 5 + k], few_r.at[s, 5 + k], y_to[k - 1]) for k in (1, 2, 3)
        ]
        for copy in copies:
            copy.start()
        return copies

    def small_x(s):
        x_out[s] = ordered_sum(y_in, s, yy)
        mb_rows = x_out.at[s, pl.ds(64, 8)]
        copies = [
            remote(x_out.at[s], x_in.at[s], few_s.at[s, 9], few_r.at[s, 9], xp),
            remote(mb_rows, mbx_in.at[s, 0], few_s.at[s, 10], few_r.at[s, 10], cp),
            remote(mb_rows, mbx_in.at[s, 1], few_s.at[s, 11], few_r.at[s, 11], dg),
        ]
        for copy in copies:
            copy.start()
        return copies

    def small_gather(s):
        ag_in[s, 0, 0:64, :] = x_out[s, 0:64, :] + x_in[s, 0:64, :]
        ag_in[s, 0, 64:96, :] = pa_sum[s] + pa_cp[s]
        copies = [
            remote(ag_in.at[s, 0], ag_in.at[s, k], few_s.at[s, 11 + k], few_r.at[s, 11 + k], z_to[k - 1])
            for k in (1, 2, 3)
        ]
        for copy in copies:
            copy.start()
        return copies

    def small_half(s):
        for p in range(4):
            k = lax.rem(z + 4 - p, 4)
            ma[32 * p : 32 * p + 32, :] = ag_in[s, k, 0:32, :]
            half_out[s, 32 * p : 32 * p + 32, :] = ag_in[s, k, 32:64, :]
            half_out[s, 128 + 32 * p : 128 + 32 * p + 32, :] = ag_in[s, k, 64:96, :]
        copy = remote(half_out.at[s], half_in.at[s], few_s.at[s, 15], few_r.at[s, 15], sib)
        copy.start()
        return copy

    def small_end(s, a, b):
        upper = pl.ds(pl.multiple_of(core * 128, 128), 128)
        lower = pl.ds(pl.multiple_of((1 - core) * 128, 128), 128)
        pc[upper, :] = half_out[s, 0:128, :]
        pc[lower, :] = half_in[s, 0:128, :]
        pa[upper, :] = half_out[s, 128:256, :]
        pa[lower, :] = half_in[s, 128:256, :]
        pb = exact(b, b, 0, 0)
        mb = (x_out[s, 64:72, :] + mbx_in[s, 0]) + (x_in[s, 64:72, :] + mbx_in[s, 1])
        hessian_a = pb * pc[...]
        hessian_b = pa[...] * pc[...]
        new_a = a - (exact(a, hessian_a, 1, 0) - ma[...]) * inverse_norm(hessian_a)
        new_b = b - (exact(b, hessian_b, 1, 0) - mb) * inverse_norm(hessian_b)
        hessian_c = pa[...] * pb
        scale = inverse_norm(hessian_c)
        pa[...] = hessian_c
        return new_a, new_b, scale

    def wait(copies):
        for copy in copies:
            copy.wait()

    khatri_rao(a0[...], b0[...])
    pl.semaphore_wait(barrier, len(partners))

    pa_copy = small_pa(0, a0[...])
    pa_copy.start()
    run(0, 0, 1, True)
    pa_copy.wait()
    pa_copy = small_pa_sum(0)
    pa_copy.start()
    run(0, 1, FIRST, True)
    load_c.wait()
    y[...] = jnp.zeros_like(y)
    gram[...] = jnp.zeros_like(gram)

    def first_y(i, carry):
        @pl.when(i >= FIRST)
        def _():
            load_t(i).wait()

        accumulate(c0, i)
        return carry

    lax.fori_loop(0, CHUNKS, first_y, 0)
    mb_copy = small_mb(0, a0[...])
    mb_copy.start()
    copies = small_pieces(0, b0[...], mb_copy)
    run(0, FIRST, SECOND)
    wait(copies)
    copies = small_y(0)
    wait(copies)
    copies = small_x(0)
    run(0, SECOND, CHUNKS)
    wait(copies)
    pa_copy.wait()
    copies = small_gather(0)
    wait(copies)
    copy = small_half(0)
    copy.wait()
    new_a, new_b, scale = small_end(0, a0[...], b0[...])
    a1[...] = new_a
    b1[...] = new_b
    khatri_rao(new_a, new_b)

    pa_copy = small_pa(1, new_a)
    pa_copy.start()
    run(1, 0, THIRD)
    pa_copy.wait()
    y[...] = jnp.zeros_like(y)
    gram[...] = jnp.zeros_like(gram)

    def second_y(i, carry):
        @pl.when(i < CHUNKS)
        def _():
            c1[own_rows(i), :] = update_c(0, i, c0, pa, scale)
            c1_to_sib(i).start()

        @pl.when(i > 0)
        def _():
            c1_to_sib(i - 1).wait()
            accumulate(c1, i - 1)

        return carry

    lax.fori_loop(0, CHUNKS + 1, second_y, 0)
    mb_copy = small_mb(1, a1[...])
    mb_copy.start()
    copies = small_pieces(1, b1[...], mb_copy)
    wait(copies)
    copies = small_y(1)
    wait(copies)
    pa_copy = small_pa_sum(1)
    pa_copy.start()
    copies = small_x(1)
    run(1, THIRD, CHUNKS)
    wait(copies)
    pa_copy.wait()
    copies = small_gather(1)
    wait(copies)
    copy = small_half(1)
    copy.wait()
    new_a, new_b, scale = small_end(1, a1[...], b1[...])
    out_a[...] = new_a
    out_b[...] = new_b

    def last_c(i, carry):
        c2[i] = update_c(1, i, c1, pa, scale)
        c2_to_sib(i).start()
        c2_out(i).start()
        return carry

    lax.fori_loop(0, CHUNKS, last_c, 0)

    def finish(i, carry):
        c2_to_sib(i).wait()
        c2_out(i).wait()
        return carry

    lax.fori_loop(0, CHUNKS, finish, 0)


def local(intensities, sample_start, scan_start, mass_start):
    unfolded = intensities.reshape(ROWS * SCANS, BINS)
    vmem = pl.BlockSpec(memory_space=pltpu.VMEM)
    anywhere = pl.BlockSpec(memory_space=pl.ANY)
    dma = pltpu.SemaphoreType.DMA
    return pl.pallas_call(
        kernel,
        out_shape=(
            jax.ShapeDtypeStruct((ROWS, RANK), F32),
            jax.ShapeDtypeStruct((SCANS, RANK), F32),
            jax.ShapeDtypeStruct((BINS, RANK), F32),
        ),
        in_specs=[anywhere, vmem, vmem, anywhere],
        out_specs=(vmem, vmem, anywhere),
        scratch_shapes=[
            pltpu.VMEM((ROWS * SCANS, BINS), F32),
            pltpu.VMEM((BINS, RANK), F32),
            pltpu.VMEM((BINS, RANK), F32),
            pltpu.VMEM((CHUNKS, HALF, RANK), F32),
            pltpu.VMEM((STEPS, CHUNKS, WIDE, RANK), F32),
            pltpu.VMEM((STEPS, CHUNKS, HALF, RANK), F32),
            pltpu.VMEM((STEPS, CHUNKS, HALF, RANK), F32),
            pltpu.VMEM((ROWS * SCANS, RANK), F32),
            pltpu.VMEM((ROWS * SCANS, RANK), BF16),
            pltpu.VMEM((ROWS * SCANS, RANK), BF16),
            pltpu.VMEM((128, RANK), F32),
            pltpu.VMEM((ROWS, RANK), F32),
            pltpu.VMEM((SCANS, RANK), F32),
            pltpu.VMEM((RANK, RANK), F32),
            pltpu.VMEM((RANK, RANK), F32),
            pltpu.VMEM((ROWS, RANK), F32),
            pltpu.VMEM((RANK, RANK), F32),
            pltpu.VMEM((STEPS, 32, RANK), F32),
            pltpu.VMEM((STEPS, 32, RANK), F32),
            pltpu.VMEM((STEPS, 32, RANK), F32),
            pltpu.VMEM((STEPS, 8, RANK), F32),
            pltpu.VMEM((STEPS, 8, RANK), F32),
            pltpu.VMEM((STEPS, 4, PIECE, RANK), F32),
            pltpu.VMEM((STEPS, 4, PIECE, RANK), F32),
            pltpu.VMEM((STEPS, 4, PIECE, RANK), F32),
            pltpu.VMEM((STEPS, PIECE, RANK), F32),
            pltpu.VMEM((STEPS, PIECE, RANK), F32),
            pltpu.VMEM((STEPS, 2, 8, RANK), F32),
            pltpu.VMEM((STEPS, 4, 96, RANK), F32),
            pltpu.VMEM((STEPS, 256, RANK), F32),
            pltpu.VMEM((STEPS, 256, RANK), F32),
            dma((CHUNKS,)),
            dma(()),
            dma((CHUNKS,)),
            dma((STEPS, CHUNKS)),
            dma((STEPS, CHUNKS)),
            dma((STEPS, CHUNKS)),
            dma((STEPS, CHUNKS)),
            dma((CHUNKS,)),
            dma((CHUNKS,)),
            dma((CHUNKS,)),
            dma((CHUNKS,)),
            dma((STEPS, 16)),
            dma((STEPS, 16)),
        ],
        compiler_params=pltpu.CompilerParams(
            collective_id=3, has_side_effects=True, vmem_limit_bytes=60 * 1024 * 1024
        ),
    )(unfolded, sample_start, scan_start, mass_start)


def solution(mesh):
    placed = (P("grp", None, "mz"), P("grp", None), P(), P("mz", None))
    return jax.shard_map(
        local,
        mesh=mesh,
        in_specs=placed,
        out_specs=(P("grp", None), P(), P("mz", None)),
        check_vma=False,
    )
```

time: 1060 us -> 130 us (0.12)
  waiting for transfers between devices: 802 us -> 0 us
  matrix products: 156 us -> 0 us
  Pallas kernels: 0 us -> 122 us
  blocking collectives: 66.3 us -> 0 us
  between operations: 18.5 us -> 0.64 us
    psum x4 -> x0, waiting for transfers between devices: 802 us -> none  [the longest x2 572 us: local(): lax.psum(jnp.einsum('ijr,jr->ir', contracted, factor_b, precision=precise...]
    dot_general x18 -> x0, matrix products: 156 us -> none  [the longest x2 57.8 us: local(): lax.dot_general(unfolded, khatri_rao, (((0,), (0,)), ((), ())), precision...]
    pallas_call x0 -> x1, Pallas kernels: none -> 122 us  [local(): pl.pallas_call(kernel, out_shape=(jax.ShapeDtypeStruct((ROWS, RANK), F32)...]
    psum x1 -> x0, blocking collectives: 66.3 us -> none  [local(): lax.psum(jnp.einsum('ijr,ir->jr', contracted, factor_a, precision=precise...]
  transfers between devices with their start and end apart: 4 -> 0, of which waited for: 4 -> 0; matrix products, arithmetic and copies ran while one was open for 6% -> 0% of each run, Pallas kernels for 0% -> 0%
where the time goes in v1:
time: 130 us
  Pallas kernels  122 us (94%)
  local copies, waits for them, and re-layouts  7.33 us (6%)
    pallas_call x1, Pallas kernels, local(): pl.pallas_call(kernel, out_shape=(jax.ShapeDtypeStruct((ROWS, RANK), F32)...  122 us
    unnamed x3, local copies, waits for them, and re-layouts  7.33 us

profile of v1, /device:TPU:1, one launch (start us, length us, event | category | flops | bytes accessed | tf_op | source)
XLA Modules:
  0.0 129.9 jit_solution(9172203960427005636)
XLA Ops:
  0.6 121.9 %shard_map.67 = (f32[128,256]{1,0:T(8,128)}, f32[8,256]{1,0:T(8,128)}, f32[4096,256]{1,0:T(8,128)}) custom-call(f32[1024,4096]{1,0:T(8,128)} %bitcast.1, f32[128,256]{1,0:T(8,128)} %a0.1, f32[8,256]{1,0:T(8,128)} %b0.1, f32[4096,256]{1,0:T(8,128)} %c_hbm.1), custom_call_target="tpu_custom_call" | custom-call | tf_op jit(solution)/shard_map/pallas_call | solution.py:362
  122.5 1.6 %copy.10 = f32[128,256]{1,0:T(8,128)} copy(f32[128,256]{1,0:T(8,128)} %get-tuple-element.6) | data formatting | bytes 262144
  124.1 1.3 copy.11
  125.4 4.5 %copy.12 = f32[4096,256]{1,0:T(8,128)} copy(f32[4096,256]{1,0:T(8,128)} %get-tuple-element.8) | data formatting | bytes 8388608

commit v2 on v1

--- a/solution.py
+++ b/solution.py
@@ -15,12 +15,13 @@
 SCANS = 8
 ROWS = 128
 BINS = 4096
-CHUNKS = 16
+CHUNKS = 8
 WIDE = BINS // CHUNKS
 HALF = WIDE // 2
-FIRST = 8
-SECOND = 10
-THIRD = 10
+FIRST = 4
+SECOND = 5
+THIRD = 4
+TAKEN_Z, TAKEN_Y, TAKEN_X, TAKEN = 0, 2, 4, 5
 PIECE = 72
 
 
@@ -48,11 +49,11 @@
 
 
 def kernel(
-    t_hbm, a0, b0, c_hbm, out_a, out_b, out_c,
-    t, c0, c1, c2, part, from_sib, from_cp, y, krh, krl, gram, a1, b1,
-    pc, pa, ma, grama, pa_in, pa_sum, pa_cp, mb_out, mb_in,
+    t_hbm, a_hbm, b_hbm, c_hbm, out_a, out_b, out_c,
+    a0, b0, t, c0, c1, part, from_sib, from_cp, y, krh, krl, gram, a1, b1,
+    pc, pa, hc, ma, grama, pa_in, pa_sum, pa_cp, pa_ag, pa_half_out, pa_half_in, mb_out, mb_in,
     pieces, z_in, y_in, x_out, x_in, mbx_in, ag_in, half_out, half_in,
-    t_sem, c_sem, o_sem, sib_s, sib_r, cp_s, cp_r, c1_s, c1_r, c2_s, c2_r, few_s, few_r,
+    t_sem, c_sem, sib_s, sib_r, cp_s, cp_r, c1_s, c1_r, c2_s, c2_r, few_s, few_r,
 ):
     g = lax.axis_index("grp")
     m = lax.axis_index("mz")
@@ -67,20 +68,22 @@
     z_to = [(g, m - z + lax.rem(z + k, 4)) for k in (1, 2, 3)]
     y_to = [(g, m + 8 * (lax.rem(yy + k, 4) - yy)) for k in (1, 2, 3)]
 
-    def load_t(i):
-        cols = pl.ds(pl.multiple_of(i * WIDE, WIDE), WIDE)
-        return pltpu.make_async_copy(t_hbm.at[:, cols], t.at[:, cols], t_sem.at[i])
-
-    load_c = pltpu.make_async_copy(c_hbm, c0, c_sem)
-    for i in range(CHUNKS):
-        load_t(i).start()
-    load_c.start()
-
     partners = [sib, cp, xp, dg, *z_to, *y_to]
     barrier = pltpu.get_barrier_semaphore()
     for partner in partners:
         pl.semaphore_signal(barrier, inc=1, device_id=partner, device_id_type=MESH)
 
+    def load_t(i):
+        cols = pl.ds(pl.multiple_of(i * WIDE, WIDE), WIDE)
+        return pltpu.make_async_copy(t_hbm.at[:, cols], t.at[:, cols], t_sem.at[i])
+
+    load_c = pltpu.make_async_copy(c_hbm, c0, c_sem)
+    load_a = pltpu.make_async_copy(a_hbm, a0, few_s.at[0, 20])
+    load_b = pltpu.make_async_copy(b_hbm, b0, few_s.at[0, 21])
+    load_a.start()
+    load_b.start()
+    load_t(0).start()
+
     def khatri_rao(a, b):
         product = (a[:, None, :] * b[None, :, :]).reshape(ROWS * SCANS, RANK)
         krh[...], krl[...] = split(product)
@@ -109,21 +112,21 @@
         return remote(c1.at[own_rows(i)], c1.at[own_rows(i)], c1_s.at[i], c1_r.at[i], sib)
 
     def c2_to_sib(i):
-        return remote(c2.at[i], out_c.at[own_rows(i)], c2_s.at[i], c2_r.at[i], sib)
-
-    def c2_out(i):
-        return pltpu.make_async_copy(c2.at[i], out_c.at[own_rows(i)], o_sem.at[i])
+        return remote(out_c.at[own_rows(i)], out_c.at[own_rows(i)], c2_s.at[i], c2_r.at[i], sib)
 
     def produce(s, i):
         part[s, i] = contract3(split(t[:, chunk(i)]), (krh[...], krl[...]), 0, 0)
         to_sib(s, i).start()
 
-    def forward(s, i):
+    def prepare(s, i):
         to_sib(s, i).wait()
         part[s, i, own] += from_sib[s, i]
+
+    def forward(s, i):
+        prepare(s, i)
         to_cp(s, i).start()
 
-    def run(s, first, last, wait_t=False):
+    def run(s, first, last, wait_t=False, then=forward):
         def body(i, carry):
             if wait_t:
                 load_t(i).wait()
@@ -131,12 +134,12 @@
 
             @pl.when(i > first)
             def _():
-                forward(s, i - 1)
+                then(s, i - 1)
 
             return carry
 
         lax.fori_loop(first, last, body, 0)
-        forward(s, last - 1)
+        then(s, last - 1)
 
     def accumulate(factor, i):
         rows = chunk(i)
@@ -145,11 +148,11 @@
         mine = split(factor[rows, pl.ds(pl.multiple_of(core * 128, 128), 128)])
         gram[...] += contract3(mine, block, 0, 0)
 
-    def update_c(s, i, source, hessian, scale):
+    def update_c(s, i, source, scale):
         to_cp(s, i).wait()
         drive = part[s, i, own] + from_cp[s, i]
         old = source[own_rows(i), :]
-        return old - (exact(old, hessian[...], 1, 0) - drive) * scale
+        return old - (exact(old, hc[s], 1, 0) - drive) * scale
 
     def small_pa(s, a):
         grama[...] = exact(a, a, 0, 0)
@@ -160,6 +163,33 @@
         mine = pl.ds(pl.multiple_of(core * 128 + z * 32, 32), 32)
         pa_sum[s] = grama[mine, :] + pa_in[s]
         return remote(pa_sum.at[s], pa_cp.at[s], few_s.at[s, 1], few_r.at[s, 1], cp)
+
+    def small_pa_gather(s):
+        pa_ag[s, 0] = pa_sum[s] + pa_cp[s]
+        copies = [
+            remote(pa_ag.at[s, 0], pa_ag.at[s, k], few_s.at[s, 15 + k], few_r.at[s, 15 + k], z_to[k - 1])
+            for k in (1, 2, 3)
+        ]
+        for copy in copies:
+            copy.start()
+        return copies
+
+    def small_pa_half(s):
+        for p in range(4):
+            pa_half_out[s, 32 * p : 32 * p + 32, :] = pa_ag[s, lax.rem(z + 4 - p, 4)]
+        copy = remote(pa_half_out.at[s], pa_half_in.at[s], few_s.at[s, 19], few_r.at[s, 19], sib)
+        copy.start()
+        return copy
+
+    upper = pl.ds(pl.multiple_of(core * 128, 128), 128)
+    lower = pl.ds(pl.multiple_of((1 - core) * 128, 128), 128)
+
+    def small_pa_end(s, b):
+        pa[upper, :] = pa_half_out[s]
+        pa[lower, :] = pa_half_in[s]
+        hessian_c = pa[...] * exact(b, b, 0, 0)
+        hc[s] = hessian_c
+        return inverse_norm(hessian_c)
 
     def small_mb(s, a):
         y3 = y[...].reshape(ROWS, SCANS, RANK)
@@ -212,8 +242,7 @@
         return copies
 
     def small_gather(s):
-        ag_in[s, 0, 0:64, :] = x_out[s, 0:64, :] + x_in[s, 0:64, :]
-        ag_in[s, 0, 64:96, :] = pa_sum[s] + pa_cp[s]
+        ag_in[s, 0] = x_out[s, 0:64, :] + x_in[s, 0:64, :]
         copies = [
             remote(ag_in.at[s, 0], ag_in.at[s, k], few_s.at[s, 11 + k], few_r.at[s, 11 + k], z_to[k - 1])
             for k in (1, 2, 3)
@@ -227,46 +256,67 @@
             k = lax.rem(z + 4 - p, 4)
             ma[32 * p : 32 * p + 32, :] = ag_in[s, k, 0:32, :]
             half_out[s, 32 * p : 32 * p + 32, :] = ag_in[s, k, 32:64, :]
-            half_out[s, 128 + 32 * p : 128 + 32 * p + 32, :] = ag_in[s, k, 64:96, :]
         copy = remote(half_out.at[s], half_in.at[s], few_s.at[s, 15], few_r.at[s, 15], sib)
         copy.start()
         return copy
 
     def small_end(s, a, b):
-        upper = pl.ds(pl.multiple_of(core * 128, 128), 128)
-        lower = pl.ds(pl.multiple_of((1 - core) * 128, 128), 128)
-        pc[upper, :] = half_out[s, 0:128, :]
-        pc[lower, :] = half_in[s, 0:128, :]
-        pa[upper, :] = half_out[s, 128:256, :]
-        pa[lower, :] = half_in[s, 128:256, :]
+        pc[upper, :] = half_out[s]
+        pc[lower, :] = half_in[s]
         pb = exact(b, b, 0, 0)
         mb = (x_out[s, 64:72, :] + mbx_in[s, 0]) + (x_in[s, 64:72, :] + mbx_in[s, 1])
         hessian_a = pb * pc[...]
         hessian_b = pa[...] * pc[...]
         new_a = a - (exact(a, hessian_a, 1, 0) - ma[...]) * inverse_norm(hessian_a)
         new_b = b - (exact(b, hessian_b, 1, 0) - mb) * inverse_norm(hessian_b)
-        hessian_c = pa[...] * pb
-        scale = inverse_norm(hessian_c)
-        pa[...] = hessian_c
-        return new_a, new_b, scale
+        return new_a, new_b
 
     def wait(copies):
         for copy in copies:
             copy.wait()
 
+    load_a.wait()
+    load_b.wait()
     khatri_rao(a0[...], b0[...])
     pl.semaphore_wait(barrier, len(partners))
 
+    def clear():
+        y[...] = jnp.zeros_like(y)
+        gram[...] = jnp.zeros_like(gram)
+
+    def take(first, last, scale):
+        def body(i, carry):
+            c1[own_rows(i), :] = update_c(0, i, c0, scale)
+            c1_to_sib(i).start()
+
+            @pl.when(i > first)
+            def _():
+                c1_to_sib(i - 1).wait()
+                accumulate(c1, i - 1)
+
+            return carry
+
+        if last > first:
+            lax.fori_loop(first, last, body, 0)
+            c1_to_sib(last - 1).wait()
+            accumulate(c1, last - 1)
+
     pa_copy = small_pa(0, a0[...])
     pa_copy.start()
-    run(0, 0, 1, True)
+    load_t(0).wait()
+    for i in range(1, CHUNKS):
+        load_t(i).start()
+    load_c.start()
+    produce(0, 0)
     pa_copy.wait()
     pa_copy = small_pa_sum(0)
     pa_copy.start()
+    forward(0, 0)
     run(0, 1, FIRST, True)
+    pa_copy.wait()
+    pa_copies = small_pa_gather(0)
     load_c.wait()
-    y[...] = jnp.zeros_like(y)
-    gram[...] = jnp.zeros_like(gram)
+    clear()
 
     def first_y(i, carry):
         @pl.when(i >= FIRST)
@@ -277,78 +327,79 @@
         return carry
 
     lax.fori_loop(0, CHUNKS, first_y, 0)
+    wait(pa_copies)
+    pa_copy = small_pa_half(0)
     mb_copy = small_mb(0, a0[...])
     mb_copy.start()
     copies = small_pieces(0, b0[...], mb_copy)
     run(0, FIRST, SECOND)
+    pa_copy.wait()
+    scale = small_pa_end(0, b0[...])
+    clear()
+    take(TAKEN_Z, TAKEN_Y, scale)
     wait(copies)
     copies = small_y(0)
+    take(TAKEN_Y, TAKEN_X, scale)
     wait(copies)
     copies = small_x(0)
     run(0, SECOND, CHUNKS)
     wait(copies)
-    pa_copy.wait()
     copies = small_gather(0)
+    take(TAKEN_X, TAKEN, scale)
     wait(copies)
     copy = small_half(0)
     copy.wait()
-    new_a, new_b, scale = small_end(0, a0[...], b0[...])
+    new_a, new_b = small_end(0, a0[...], b0[...])
     a1[...] = new_a
     b1[...] = new_b
     khatri_rao(new_a, new_b)
 
     pa_copy = small_pa(1, new_a)
     pa_copy.start()
-    run(1, 0, THIRD)
-    pa_copy.wait()
-    y[...] = jnp.zeros_like(y)
-    gram[...] = jnp.zeros_like(gram)
-
-    def second_y(i, carry):
-        @pl.when(i < CHUNKS)
-        def _():
-            c1[own_rows(i), :] = update_c(0, i, c0, pa, scale)
-            c1_to_sib(i).start()
-
-        @pl.when(i > 0)
-        def _():
-            c1_to_sib(i - 1).wait()
-            accumulate(c1, i - 1)
-
-        return carry
-
-    lax.fori_loop(0, CHUNKS + 1, second_y, 0)
+    produce(1, 0)
+    pa_copy.wait()
+    pa_copy = small_pa_sum(1)
+    pa_copy.start()
+    forward(1, 0)
+    run(1, 1, THIRD)
+    take(TAKEN, CHUNKS, scale)
+    pa_copy.wait()
+    pa_copies = small_pa_gather(1)
     mb_copy = small_mb(1, a1[...])
     mb_copy.start()
     copies = small_pieces(1, b1[...], mb_copy)
+    run(1, THIRD, CHUNKS - 2, then=prepare)
+    wait(pa_copies)
+    pa_copy = small_pa_half(1)
     wait(copies)
     copies = small_y(1)
-    wait(copies)
-    pa_copy = small_pa_sum(1)
-    pa_copy.start()
+    run(1, CHUNKS - 2, CHUNKS, then=prepare)
+    pa_copy.wait()
+    scale = small_pa_end(1, b1[...])
+    wait(copies)
     copies = small_x(1)
-    run(1, THIRD, CHUNKS)
-    wait(copies)
-    pa_copy.wait()
+    for i in range(THIRD, CHUNKS):
+        to_cp(1, i).start()
+
+    def last_c(i, carry):
+        out_c[own_rows(i), :] = update_c(1, i, c1, scale)
+        c2_to_sib(i).start()
+        return carry
+
+    lax.fori_loop(0, 2, last_c, 0)
+    wait(copies)
     copies = small_gather(1)
+    lax.fori_loop(2, 3, last_c, 0)
     wait(copies)
     copy = small_half(1)
     copy.wait()
-    new_a, new_b, scale = small_end(1, a1[...], b1[...])
+    new_a, new_b = small_end(1, a1[...], b1[...])
     out_a[...] = new_a
     out_b[...] = new_b
-
-    def last_c(i, carry):
-        c2[i] = update_c(1, i, c1, pa, scale)
-        c2_to_sib(i).start()
-        c2_out(i).start()
-        return carry
-
-    lax.fori_loop(0, CHUNKS, last_c, 0)
+    lax.fori_loop(3, CHUNKS, last_c, 0)
 
     def finish(i, carry):
         c2_to_sib(i).wait()
-        c2_out(i).wait()
         return carry
 
     lax.fori_loop(0, CHUNKS, finish, 0)
@@ -362,17 +413,18 @@
     return pl.pallas_call(
         kernel,
         out_shape=(
-            jax.ShapeDtypeStruct((ROWS, RANK), F32),
-            jax.ShapeDtypeStruct((SCANS, RANK), F32),
-            jax.ShapeDtypeStruct((BINS, RANK), F32),
+            pltpu.VMEM((ROWS, RANK), F32),
+            pltpu.VMEM((SCANS, RANK), F32),
+            pltpu.VMEM((BINS, RANK), F32),
         ),
-        in_specs=[anywhere, vmem, vmem, anywhere],
-        out_specs=(vmem, vmem, anywhere),
+        in_specs=[pl.BlockSpec(memory_space=pltpu.HBM)] * 4,
+        out_specs=(vmem, vmem, vmem),
         scratch_shapes=[
+            pltpu.VMEM((ROWS, RANK), F32),
+            pltpu.VMEM((SCANS, RANK), F32),
             pltpu.VMEM((ROWS * SCANS, BINS), F32),
             pltpu.VMEM((BINS, RANK), F32),
             pltpu.VMEM((BINS, RANK), F32),
-            pltpu.VMEM((CHUNKS, HALF, RANK), F32),
             pltpu.VMEM((STEPS, CHUNKS, WIDE, RANK), F32),
             pltpu.VMEM((STEPS, CHUNKS, HALF, RANK), F32),
             pltpu.VMEM((STEPS, CHUNKS, HALF, RANK), F32),
@@ -384,11 +436,15 @@
             pltpu.VMEM((SCANS, RANK), F32),
             pltpu.VMEM((RANK, RANK), F32),
             pltpu.VMEM((RANK, RANK), F32),
+            pltpu.VMEM((STEPS, RANK, RANK), F32),
             pltpu.VMEM((ROWS, RANK), F32),
             pltpu.VMEM((RANK, RANK), F32),
             pltpu.VMEM((STEPS, 32, RANK), F32),
             pltpu.VMEM((STEPS, 32, RANK), F32),
             pltpu.VMEM((STEPS, 32, RANK), F32),
+            pltpu.VMEM((STEPS, 4, 32, RANK), F32),
+            pltpu.VMEM((STEPS, 128, RANK), F32),
+            pltpu.VMEM((STEPS, 128, RANK), F32),
             pltpu.VMEM((STEPS, 8, RANK), F32),
             pltpu.VMEM((STEPS, 8, RANK), F32),
             pltpu.VMEM((STEPS, 4, PIECE, RANK), F32),
@@ -397,12 +453,11 @@
             pltpu.VMEM((STEPS, PIECE, RANK), F32),
             pltpu.VMEM((STEPS, PIECE, RANK), F32),
             pltpu.VMEM((STEPS, 2, 8, RANK), F32),
-            pltpu.VMEM((STEPS, 4, 96, RANK), F32),
-            pltpu.VMEM((STEPS, 256, RANK), F32),
-            pltpu.VMEM((STEPS, 256, RANK), F32),
+            pltpu.VMEM((STEPS, 4, 64, RANK), F32),
+            pltpu.VMEM((STEPS, 128, RANK), F32),
+            pltpu.VMEM((STEPS, 128, RANK), F32),
             dma((CHUNKS,)),
             dma(()),
-            dma((CHUNKS,)),
             dma((STEPS, CHUNKS)),
             dma((STEPS, CHUNKS)),
             dma((STEPS, CHUNKS)),
@@ -411,11 +466,11 @@
             dma((CHUNKS,)),
             dma((CHUNKS,)),
             dma((CHUNKS,)),
-            dma((STEPS, 16)),
-            dma((STEPS, 16)),
+            dma((STEPS, 22)),
+            dma((STEPS, 22)),
         ],
         compiler_params=pltpu.CompilerParams(
-            collective_id=3, has_side_effects=True, vmem_limit_bytes=60 * 1024 * 1024
+            collective_id=3, has_side_effects=True, vmem_limit_bytes=54 * 1024 * 1024
         ),
     )(unfolded, sample_start, scan_start, mass_start)
 

time: 130 us -> 115 us (0.88)
  Pallas kernels: 122 us -> 111 us
  local copies, waits for them, and re-layouts: 7.33 us -> 3.27 us
    pallas_call x1, Pallas kernels: 122 us -> 111 us  [local(): pl.pallas_call(kernel, out_shape=(pltpu.VMEM((ROWS, RANK), F32), pltpu.VM...]
    unnamed x3, local copies, waits for them, and re-layouts: 7.33 us -> 3.27 us
where the time goes in v2:
time: 115 us
  Pallas kernels  111 us (97%)
  local copies, waits for them, and re-layouts  3.27 us (3%)
    pallas_call x1, Pallas kernels, local(): pl.pallas_call(kernel, out_shape=(pltpu.VMEM((ROWS, RANK), F32), pltpu.VM...  111 us
    unnamed x3, local copies, waits for them, and re-layouts  3.27 us

profile of v2, /device:TPU:1, one launch (start us, length us, event | category | flops | bytes accessed | tf_op | source)
XLA Modules:
  0.0 114.8 jit_solution(18056385917840622586)
XLA Ops:
  0.6 110.9 %shard_map.67 = (f32[128,256]{1,0:T(8,128)S(1)}, f32[8,256]{1,0:T(8,128)S(1)}, f32[4096,256]{1,0:T(8,128)S(1)}) custom-call(f32[1024,4096]{1,0:T(8,128)} %bitcast.1, f32[128,256]{1,0:T(8,128)} %a_hbm.1, f32[8,256]{1,0:T(8,128)} %b_hbm.1, f32[4096,256]{1,0:T(8,128)} %c_hbm.1), custom_call_target="tpu_custom_call" | custom-call | tf_op jit(solution)/shard_map/pallas_call | solution.py:413
  111.5 0.7 copy.10
  112.2 0.6 copy.11
  112.8 2.0 %copy.12 = f32[4096,256]{1,0:T(8,128)} copy(f32[4096,256]{1,0:T(8,128)S(1)} %get-tuple-element.5) | data formatting | bytes 8388608

commit v3 on v2

--- a/solution.py
+++ b/solution.py
@@ -18,10 +18,12 @@
 CHUNKS = 8
 WIDE = BINS // CHUNKS
 HALF = WIDE // 2
+SPREAD = (False, True)
 FIRST = 4
 SECOND = 5
+PA_CP, PA_HALF = 3, 7
 THIRD = 4
-TAKEN_Z, TAKEN_Y, TAKEN_X, TAKEN = 0, 2, 4, 5
+TAKEN_Z, TAKEN_Y, TAKEN_X, TAKEN = 0, 2, 3, 3
 PIECE = 72
 
 
@@ -52,7 +54,7 @@
     t_hbm, a_hbm, b_hbm, c_hbm, out_a, out_b, out_c,
     a0, b0, t, c0, c1, part, from_sib, from_cp, y, krh, krl, gram, a1, b1,
     pc, pa, hc, ma, grama, pa_in, pa_sum, pa_cp, pa_ag, pa_half_out, pa_half_in, mb_out, mb_in,
-    pieces, z_in, y_in, x_out, x_in, mbx_in, ag_in, half_out, half_in,
+    pieces, z_in, y_in, y_parts, y_some, y_ag, x_out, x_in, mbx_in, ag_in, half_out, half_in,
     t_sem, c_sem, sib_s, sib_r, cp_s, cp_r, c1_s, c1_r, c2_s, c2_r, few_s, few_r,
 ):
     g = lax.axis_index("grp")
@@ -126,11 +128,13 @@
         prepare(s, i)
         to_cp(s, i).start()
 
-    def run(s, first, last, wait_t=False, then=forward):
+    def run(s, first, last, wait_t=False, then=forward, also=None):
         def body(i, carry):
             if wait_t:
                 load_t(i).wait()
             produce(s, i)
+            if also is not None:
+                also(i)
 
             @pl.when(i > first)
             def _():
@@ -164,12 +168,15 @@
         pa_sum[s] = grama[mine, :] + pa_in[s]
         return remote(pa_sum.at[s], pa_cp.at[s], few_s.at[s, 1], few_r.at[s, 1], cp)
 
-    def small_pa_gather(s):
-        pa_ag[s, 0] = pa_sum[s] + pa_cp[s]
-        copies = [
+    def pa_gather_copies(s):
+        return [
             remote(pa_ag.at[s, 0], pa_ag.at[s, k], few_s.at[s, 15 + k], few_r.at[s, 15 + k], z_to[k - 1])
             for k in (1, 2, 3)
         ]
+
+    def small_pa_gather(s):
+        pa_ag[s, 0] = pa_sum[s] + pa_cp[s]
+        copies = pa_gather_copies(s)
         for copy in copies:
             copy.start()
         return copies
@@ -221,7 +228,23 @@
         return total
 
     def small_y(s):
-        y_in[s, 0] = ordered_sum(z_in, s, z)
+        total = ordered_sum(z_in, s, z)
+        if SPREAD[s]:
+            for p in range(4):
+                y_parts[s, p, 0:8, :] = total[8 * p : 8 * p + 8]
+                y_parts[s, p, 8:16, :] = total[32 + 8 * p : 40 + 8 * p]
+                y_parts[s, p, 16:24, :] = total[64:72]
+            y_some[s, 0] = y_parts[s, yy]
+            copies = [
+                remote(
+                    y_parts.at[s, lax.rem(yy + k, 4)], y_some.at[s, k], few_s.at[s, 5 + k], few_r.at[s, 5 + k], y_to[k - 1]
+                )
+                for k in (1, 2, 3)
+            ]
+            for copy in copies:
+                copy.start()
+            return copies
+        y_in[s, 0] = total
         copies = [
             remote(y_in.at[s, 0], y_in.at[s, k], few_s.at[s, 5 + k], few_r.at[s, 5 + k], y_to[k - 1]) for k in (1, 2, 3)
         ]
@@ -230,10 +253,15 @@
         return copies
 
     def small_x(s):
-        x_out[s] = ordered_sum(y_in, s, yy)
+        if SPREAD[s]:
+            x_out[s, 48:72, :] = ordered_sum(y_some, s, yy)
+            sent = pl.ds(48, 24)
+        else:
+            x_out[s] = ordered_sum(y_in, s, yy)
+            sent = pl.ds(0, PIECE)
         mb_rows = x_out.at[s, pl.ds(64, 8)]
         copies = [
-            remote(x_out.at[s], x_in.at[s], few_s.at[s, 9], few_r.at[s, 9], xp),
+            remote(x_out.at[s, sent], x_in.at[s, sent], few_s.at[s, 9], few_r.at[s, 9], xp),
             remote(mb_rows, mbx_in.at[s, 0], few_s.at[s, 10], few_r.at[s, 10], cp),
             remote(mb_rows, mbx_in.at[s, 1], few_s.at[s, 11], few_r.at[s, 11], dg),
         ]
@@ -241,8 +269,23 @@
             copy.start()
         return copies
 
+    def small_spread(s):
+        y_ag[s, 0] = x_out[s, 48:64, :] + x_in[s, 48:64, :]
+        copies = [
+            remote(y_ag.at[s, 0], y_ag.at[s, k], few_s.at[s, 21 + k], few_r.at[s, 21 + k], y_to[k - 1]) for k in (1, 2, 3)
+        ]
+        for copy in copies:
+            copy.start()
+        return copies
+
     def small_gather(s):
-        ag_in[s, 0] = x_out[s, 0:64, :] + x_in[s, 0:64, :]
+        if SPREAD[s]:
+            for p in range(4):
+                block = y_ag[s, lax.rem(yy + 4 - p, 4)]
+                ag_in[s, 0, 8 * p : 8 * p + 8, :] = block[0:8]
+                ag_in[s, 0, 32 + 8 * p : 40 + 8 * p, :] = block[8:16]
+        else:
+            ag_in[s, 0] = x_out[s, 0:64, :] + x_in[s, 0:64, :]
         copies = [
             remote(ag_in.at[s, 0], ag_in.at[s, k], few_s.at[s, 11 + k], few_r.at[s, 11 + k], z_to[k - 1])
             for k in (1, 2, 3)
@@ -286,8 +329,10 @@
 
     def take(first, last, scale):
         def body(i, carry):
-            c1[own_rows(i), :] = update_c(0, i, c0, scale)
-            c1_to_sib(i).start()
+            @pl.when(i < last)
+            def _():
+                c1[own_rows(i), :] = update_c(0, i, c0, scale)
+                c1_to_sib(i).start()
 
             @pl.when(i > first)
             def _():
@@ -296,25 +341,24 @@
 
             return carry
 
-        if last > first:
-            lax.fori_loop(first, last, body, 0)
-            c1_to_sib(last - 1).wait()
-            accumulate(c1, last - 1)
-
-    pa_copy = small_pa(0, a0[...])
-    pa_copy.start()
+        lax.fori_loop(first, last + 1, body, 0)
+
     load_t(0).wait()
     for i in range(1, CHUNKS):
         load_t(i).start()
     load_c.start()
     produce(0, 0)
-    pa_copy.wait()
-    pa_copy = small_pa_sum(0)
+    pa_copy = small_pa(0, a0[...])
     pa_copy.start()
     forward(0, 0)
-    run(0, 1, FIRST, True)
-    pa_copy.wait()
-    pa_copies = small_pa_gather(0)
+
+    def pa_on(i):
+        @pl.when(i == 1)
+        def _():
+            pa_copy.wait()
+            small_pa_sum(0).start()
+
+    run(0, 1, FIRST, True, also=pa_on)
     load_c.wait()
     clear()
 
@@ -324,11 +368,21 @@
             load_t(i).wait()
 
         accumulate(c0, i)
+
+        @pl.when(i == PA_CP)
+        def _():
+            remote(pa_sum.at[0], pa_cp.at[0], few_s.at[0, 1], few_r.at[0, 1], cp).wait()
+            small_pa_gather(0)
+
+        @pl.when(i == PA_HALF)
+        def _():
+            wait(pa_gather_copies(0))
+            small_pa_half(0)
+
         return carry
 
     lax.fori_loop(0, CHUNKS, first_y, 0)
-    wait(pa_copies)
-    pa_copy = small_pa_half(0)
+    pa_copy = remote(pa_half_out.at[0], pa_half_in.at[0], few_s.at[0, 19], few_r.at[0, 19], sib)
     mb_copy = small_mb(0, a0[...])
     mb_copy.start()
     copies = small_pieces(0, b0[...], mb_copy)
@@ -344,8 +398,10 @@
     copies = small_x(0)
     run(0, SECOND, CHUNKS)
     wait(copies)
+    if SPREAD[0]:
+        copies = small_spread(0)
+        wait(copies)
     copies = small_gather(0)
-    take(TAKEN_X, TAKEN, scale)
     wait(copies)
     copy = small_half(0)
     copy.wait()
@@ -386,10 +442,12 @@
         c2_to_sib(i).start()
         return carry
 
-    lax.fori_loop(0, 2, last_c, 0)
-    wait(copies)
+    lax.fori_loop(0, 3, last_c, 0)
+    wait(copies)
+    if SPREAD[1]:
+        copies = small_spread(1)
+        wait(copies)
     copies = small_gather(1)
-    lax.fori_loop(2, 3, last_c, 0)
     wait(copies)
     copy = small_half(1)
     copy.wait()
@@ -450,6 +508,9 @@
             pltpu.VMEM((STEPS, 4, PIECE, RANK), F32),
             pltpu.VMEM((STEPS, 4, PIECE, RANK), F32),
             pltpu.VMEM((STEPS, 4, PIECE, RANK), F32),
+            pltpu.VMEM((STEPS, 4, 24, RANK), F32),
+            pltpu.VMEM((STEPS, 4, 24, RANK), F32),
+            pltpu.VMEM((STEPS, 4, 16, RANK), F32),
             pltpu.VMEM((STEPS, PIECE, RANK), F32),
             pltpu.VMEM((STEPS, PIECE, RANK), F32),
             pltpu.VMEM((STEPS, 2, 8, RANK), F32),
@@ -466,11 +527,11 @@
             dma((CHUNKS,)),
             dma((CHUNKS,)),
             dma((CHUNKS,)),
-            dma((STEPS, 22)),
-            dma((STEPS, 22)),
+            dma((STEPS, 26)),
+            dma((STEPS, 26)),
         ],
         compiler_params=pltpu.CompilerParams(
-            collective_id=3, has_side_effects=True, vmem_limit_bytes=54 * 1024 * 1024
+            collective_id=3, has_side_effects=True, vmem_limit_bytes=55 * 1024 * 1024
         ),
     )(unfolded, sample_start, scan_start, mass_start)
 

time: 115 us -> 114 us (level)
    pallas_call x1, Pallas kernels: 111 us -> 110 us  [local(): pl.pallas_call(kernel, out_shape=(pltpu.VMEM((ROWS, RANK), F32), pltpu.VM...]
where the time goes in v3:
time: 114 us
  Pallas kernels  110 us (96%)
  local copies, waits for them, and re-layouts  3.27 us (3%)
    pallas_call x1, Pallas kernels, local(): pl.pallas_call(kernel, out_shape=(pltpu.VMEM((ROWS, RANK), F32), pltpu.VM...  110 us
    unnamed x3, local copies, waits for them, and re-layouts  3.27 us

profile of v3, /device:TPU:1, one launch (start us, length us, event | category | flops | bytes accessed | tf_op | source)
XLA Modules:
  0.0 113.6 jit_solution(17682756759313147249)
XLA Ops:
  0.6 109.7 %shard_map.67 = (f32[128,256]{1,0:T(8,128)S(1)}, f32[8,256]{1,0:T(8,128)S(1)}, f32[4096,256]{1,0:T(8,128)S(1)}) custom-call(f32[1024,4096]{1,0:T(8,128)} %bitcast.1, f32[128,256]{1,0:T(8,128)} %a_hbm.1, f32[8,256]{1,0:T(8,128)} %b_hbm.1, f32[4096,256]{1,0:T(8,128)} %c_hbm.1), custom_call_target="tpu_custom_call" | custom-call | tf_op jit(solution)/shard_map/pallas_call | solution.py:471
  110.3 0.7 copy.10
  111.0 0.6 copy.11
  111.6 2.0 %copy.12 = f32[4096,256]{1,0:T(8,128)} copy(f32[4096,256]{1,0:T(8,128)S(1)} %get-tuple-element.5) | data formatting | bytes 8388608

commit v4 on v3

--- a/solution.py
+++ b/solution.py
@@ -410,13 +410,13 @@
     b1[...] = new_b
     khatri_rao(new_a, new_b)
 
+    produce(1, 0)
     pa_copy = small_pa(1, new_a)
     pa_copy.start()
-    produce(1, 0)
+    forward(1, 0)
     pa_copy.wait()
     pa_copy = small_pa_sum(1)
     pa_copy.start()
-    forward(1, 0)
     run(1, 1, THIRD)
     take(TAKEN, CHUNKS, scale)
     pa_copy.wait()

time: 114 us -> 114 us (level)
  no operation moved by 1% of the time
where the time goes in v4:
time: 114 us
  Pallas kernels  110 us (96%)
  local copies, waits for them, and re-layouts  3.27 us (3%)
    pallas_call x1, Pallas kernels, local(): pl.pallas_call(kernel, out_shape=(pltpu.VMEM((ROWS, RANK), F32), pltpu.VM...  110 us
    unnamed x3, local copies, waits for them, and re-layouts  3.27 us

profile of v4, /device:TPU:1, one launch (start us, length us, event | category | flops | bytes accessed | tf_op | source)
XLA Modules:
  0.0 113.6 jit_solution(8126204241098005349)
XLA Ops:
  0.6 109.7 %shard_map.67 = (f32[128,256]{1,0:T(8,128)S(1)}, f32[8,256]{1,0:T(8,128)S(1)}, f32[4096,256]{1,0:T(8,128)S(1)}) custom-call(f32[1024,4096]{1,0:T(8,128)} %bitcast.1, f32[128,256]{1,0:T(8,128)} %a_hbm.1, f32[8,256]{1,0:T(8,128)} %b_hbm.1, f32[4096,256]{1,0:T(8,128)} %c_hbm.1), custom_call_target="tpu_custom_call" | custom-call | tf_op jit(solution)/shard_map/pallas_call | solution.py:471
  110.3 0.7 copy.10
  111.0 0.6 copy.11
  111.6 2.0 %copy.12 = f32[4096,256]{1,0:T(8,128)} copy(f32[4096,256]{1,0:T(8,128)S(1)} %get-tuple-element.5) | data formatting | bytes 8388608
